TPU v7x, 256 devices: a whole 4x4x8 slice. The times are simulated.
256 devices in a mesh: cluster: 4 (over x), sub: 64 (over y, z, core).
Axes of the slice: x: 4, y: 4, z: 8, core: 2. Of those that a mesh axis runs over, the one named last changes fastest.
Arguments:
- dual_ops: float32 [262144, 1024], P(('cluster', 'sub')), may hold values from -21 to 21, as said below
- boundary_solve_blocks: float32 [262144, 1024], P(('cluster', 'sub')), may hold values from -21 to 21, as said below
- rigid_images: float32 [1536, 1024], P(('cluster', 'sub')), may hold values from -0.1875 to 0.1875
- coarse_rows: float32 [1536, 1536], P(('cluster', 'sub')), may hold values from -1.5 to 1.5, as said below
- gap_raw: float32 [262144, 256], P(('cluster', 'sub')), may hold values from -12 to 12
- row_maps: int32 [256, 2, 128], P(('cluster', 'sub')), may hold values from 0 to 1023, as said below
Outputs:
- multipliers: float32 [262144, 256], P(('cluster', 'sub'))
- residual: float32 [262144, 256], P(('cluster', 'sub'))
- norms: float32 [2, 256], replicated
Inputs may be any that keep to these rules, and one draw needn't show every extreme that they name: `row_maps`: A subdomain's 2 * 128 row numbers all differ; its second list faces the first list of the next subdomain, row by row. `dual_ops`: each block of a subdomain is symmetric positive definite. `boundary_solve_blocks`: each block of a subdomain is symmetric positive definite. `coarse_rows`: Symmetric.
All inputs are finite; a program needn't handle non-finite values.
Results may differ from a plain program's by a relative error of at most 0.0003.
Values sent between devices are 32-bit elements; how exact they have to be, the bound alone decides.
No kernel may reach another device: no remote copies, remote signals or barrier semaphores. Data moves between devices by JAX's collectives and lax.ppermute only.
A program may use at most 64 MiB of HBM per device.

v0:
```python
import jax
import jax.numpy as jnp
from jax import lax
from jax.sharding import Mesh
from jax.sharding import PartitionSpec as P

ITERS = 2
CLUSTER_SUB = ("cluster", "sub_0", "sub_1", "sub_2")
SUB = ("sub_0", "sub_1", "sub_2")
finest_tier = lax.Precision.HIGHEST


def passed_along(value, axis, steps):
    count = lax.axis_size(axis)
    initial, last = (max(0, -steps), min(count, count - steps))
    return lax.ppermute(value, axis, [(source, source + steps) for source in range(initial, last)])


def from_everyone(array, axis):
    copies = jnp.broadcast_to(array, (lax.axis_size(axis), *array.shape))
    return lax.all_to_all(copies, axis, split_axis=0, concat_axis=0, tiled=True)


def laid_out(parts, dim):
    shape = list(parts.shape[1:])
    shape[dim] *= parts.shape[0]
    return jnp.moveaxis(parts, 0, dim).reshape(shape)


def gathered_copies(array, axis, dim):
    parts = from_everyone(array, axis)
    return laid_out(parts, dim)


def by_axis(array, axes):
    for axis in axes:
        array = lax.psum(array, axis)
    return array


def shards(dual_ops, boundary_solve_blocks, rigid_images, coarse_rows, gap_raw, row_maps):
    processor_count = lax.axis_size(CLUSTER_SUB)
    chain_place = lax.axis_index(CLUSTER_SUB)
    left_neighbour_rows = row_maps[0, 0]
    right_neighbour_rows = row_maps[0, 1]
    local_rows = gap_raw.shape[0]
    weight = jnp.ones((local_rows,), jnp.float32)
    weight = weight.at[left_neighbour_rows].set(
        jnp.where(chain_place > 0, 0.5, 1.0).astype(jnp.float32)
    )
    weight = weight.at[right_neighbour_rows].set(
        jnp.where(chain_place < processor_count - 1, 0.5, 1.0).astype(jnp.float32)
    )
    interface_weights = weight[:, None]

    def assemble_dual(deformation_vector):
        outgoing_right = deformation_vector[right_neighbour_rows]
        outgoing_left = deformation_vector[left_neighbour_rows]
        from_left = passed_along(outgoing_right, CLUSTER_SUB, 1)
        from_right = passed_along(outgoing_left, CLUSTER_SUB, -1)
        return (
            deformation_vector.at[left_neighbour_rows]
            .add(from_left)
            .at[right_neighbour_rows]
            .add(from_right)
        )

    def gather_onto_subdomain_vector(back_rows):
        outgoing_right = back_rows[right_neighbour_rows]
        outgoing_left = back_rows[left_neighbour_rows]
        from_left = passed_along(outgoing_right, CLUSTER_SUB, 1)
        from_right = passed_along(outgoing_left, CLUSTER_SUB, -1)
        return (
            back_rows.at[left_neighbour_rows]
            .add(from_left)
            .at[right_neighbour_rows]
            .add(from_right)
        )

    def coarse_fold(piece):
        return jnp.dot(
            coarse_rows, piece, precision=finest_tier, preferred_element_type=jnp.float32
        )

    def project(deformation_vector, partial_value):
        kernel_basis_matrix = jnp.dot(
            rigid_images,
            deformation_vector,
            precision=finest_tier,
            preferred_element_type=jnp.float32,
        )
        nearby = gathered_copies(kernel_basis_matrix, SUB, 0)
        load_amounts = coarse_fold(gathered_copies(nearby, "cluster", 0))
        total = by_axis(partial_value, CLUSTER_SUB)
        back_rows = jnp.einsum("km,kr->mr", rigid_images, load_amounts, precision=finest_tier)
        return (deformation_vector - gather_onto_subdomain_vector(back_rows), total)

    residual = assemble_dual(gap_raw)
    multipliers = jnp.zeros_like(gap_raw)
    search_direction = multipliers
    previous_norm = jnp.ones((gap_raw.shape[1],), jnp.float32)
    norm_list = []
    for iteration in range(ITERS):
        norm_part = jnp.sum(interface_weights * residual * residual, axis=0)
        projected_residual, squared_length_sum = project(residual, norm_part)
        norm_list.append(squared_length_sum)
        local_contributions = jnp.dot(
            boundary_solve_blocks,
            interface_weights * projected_residual,
            precision=finest_tier,
            preferred_element_type=jnp.float32,
        )
        smoothed = interface_weights * assemble_dual(local_contributions)
        precond_part = jnp.sum(interface_weights * projected_residual * smoothed, axis=0)
        update, precond_norm = project(smoothed, precond_part)
        if iteration == 0:
            search_direction = update
        else:
            search_direction = update + precond_norm / previous_norm * search_direction
        rigid_image = assemble_dual(
            jnp.dot(
                dual_ops,
                search_direction,
                precision=finest_tier,
                preferred_element_type=jnp.float32,
            )
        )
        bending = by_axis(
            jnp.sum(interface_weights * search_direction * rigid_image, axis=0), CLUSTER_SUB
        )
        step_size = precond_norm / bending
        multipliers = multipliers + step_size * search_direction
        residual = residual - step_size * rigid_image
        previous_norm = precond_norm
    return (multipliers, residual, jnp.stack(norm_list))


def solution(mesh):
    split = Mesh(
        mesh.devices.reshape(mesh.shape["cluster"], 4, 8, 2), ("cluster", "sub_0", "sub_1", "sub_2")
    )
    in_specs = (
        P(CLUSTER_SUB, None),
        P(CLUSTER_SUB, None),
        P(CLUSTER_SUB, None),
        P(CLUSTER_SUB, None),
        P(CLUSTER_SUB, None),
        P(CLUSTER_SUB, None, None),
    )
    out_specs = (P(CLUSTER_SUB, None), P(CLUSTER_SUB, None), P())
    return jax.shard_map(
        shards, mesh=split, in_specs=in_specs, out_specs=out_specs, check_vma=False
    )
```

profile of v0, /device:TPU:1, one launch (start us, length us, event | category | flops | bytes accessed | tf_op | source)
XLA Modules:
  0.0 553.5 jit_solution(15395506081670248507)
XLA Ops:
  17.0 29.4 %all_to_all.40 = f32[64,6,256]{2,1,0:T(8,128)S(1)} all-to-all(f32[64,6,256]{2,1,0:T(8,128)S(1)} %broadcast_in_dim.25), channel_id=1, replica_groups=mesh['cluster'=4,'sub_0'=4,'sub_1'=8,'sub_2'=2] {'sub_0','sub_1','sub_2'}, dimensions={0} | all-to-all | bytes 786432 | tf_op jit(solution)/shard_map/all_to_all | solution.py:21
  46.6 24.1 %all_to_all.41 = f32[4,384,256]{2,1,0:T(8,128)S(1)} all-to-all(f32[4,384,256]{2,1,0:T(8,128)S(1)} %broadcast_in_dim.26), channel_id=1, replica_groups=mesh['cluster'=4,'sub_0'=4,'sub_1'=8,'sub_2'=2] {'cluster'}, dimensions={0} | all-to-all | bytes 3145728 | tf_op jit(solution)/shard_map/all_to_all | solution.py:21
  86.5 13.1 %scatter_fusion.4 = f32[1024,256]{1,0:T(8,128)S(1)} fusion(f32[1024,256]{1,0:T(8,128)S(1)} %scatter_fusion.3, s32[128]{0:T(128)S(1)} %get-tuple-element.30, f32[128,256]{1,0:T(8,128)S(1)} %collective-permute-done.3), kind=kCustom, calls=%fused_computation.23 | custom fusion | flops 32768 | bytes 393728 | tf_op jit(solution)/shard_map/scatter-add | solution.py:77
  99.6 10.3 %convolution_bitcast_fusion.6 = f32[1024,256]{0,1:T(8,128)} fusion(f32[1024,1024]{1,0:T(8,128)} %param.7, f32[1024,256]{1,0:T(8,128)S(1)} %scatter_fusion.2, f32[1024,256]{1,0:T(8,128)S(1)} %scatter_fusion.4, f32[1024]{0:T(1024)S(1)} %scatter_fusion), kind=kOutput, calls=%fused_computation.46 | convolution fusion | flops 3221749760 | bytes 7344128 | tf_op jit(solution)/shard_map/dot_general | solution.py:107
  126.2 31.7 %all_to_all.42 = f32[64,6,256]{2,1,0:T(8,128)} all-to-all(f32[64,6,256]{2,1,0:T(8,128)S(1)} %broadcast_in_dim.27), channel_id=1, replica_groups=mesh['cluster'=4,'sub_0'=4,'sub_1'=8,'sub_2'=2] {'sub_0','sub_1','sub_2'}, dimensions={0} | all-to-all | bytes 786432 | tf_op jit(solution)/shard_map/all_to_all | solution.py:21
  160.9 23.2 %all_to_all.43 = f32[4,384,256]{2,1,0:T(8,128)S(1)} all-to-all(f32[4,384,256]{2,1,0:T(8,128)S(1)} %broadcast_in_dim.28), channel_id=1, replica_groups=mesh['cluster'=4,'sub_0'=4,'sub_1'=8,'sub_2'=2] {'cluster'}, dimensions={0} | all-to-all | bytes 3145728 | tf_op jit(solution)/shard_map/all_to_all | solution.py:21
  213.1 10.3 %convolution_bitcast_fusion.4 = f32[1024,256]{0,1:T(8,128)} fusion(f32[1024,256]{1,0:T(8,128)S(1)} %multiply_subtract_fusion.2, f32[1024,1024]{1,0:T(8,128)} %param.6), kind=kOutput, calls=%fused_computation.44 | convolution fusion | flops 3221225472 | bytes 6291456 | tf_op jit(solution)/shard_map/dot_general | solution.py:121
  245.4 9.1 %all-reduce.5 = (f32[256]{0:T(256)S(1)}, f32[256]{0:T(256)S(1)}) all-reduce(f32[256]{0:T(256)S(1)} %get-tuple-element.4, f32[256]{0:T(256)S(1)} %get-tuple-element.7), channel_id=1, replica_groups=mesh['cluster'=4,'sub_0'=4,'sub_1'=8,'sub_2'=2] {'cluster'}, use_global_device_ids=true, to_apply=%region_9.10 | all-reduce | flops 512 | bytes 4096 | tf_op jit(solution)/shard_map/psum | solution.py:37
  254.5 6.5 %all-reduce.3 = (f32[256]{0:T(256)S(1)}, f32[256]{0:T(256)S(1)}) all-reduce(f32[256]{0:T(256)S(1)} %get-tuple-element.21, f32[256]{0:T(256)S(1)} %get-tuple-element.22), channel_id=1, replica_groups=mesh['cluster'=4,'sub_0'=4,'sub_1'=8,'sub_2'=2] {'sub_0'}, use_global_device_ids=true, to_apply=%region_10.11 | all-reduce | flops 512 | bytes 4096 | tf_op jit(solution)/shard_map/psum | solution.py:37
  261.0 19.6 %all-reduce.1 = (f32[256]{0:T(256)S(1)}, f32[256]{0:T(256)S(1)}) all-reduce(f32[256]{0:T(256)S(1)} %get-tuple-element.16, f32[256]{0:T(256)S(1)} %get-tuple-element.17), channel_id=1, replica_groups=mesh['cluster'=4,'sub_0'=4,'sub_1'=8,'sub_2'=2] {'sub_1'}, use_global_device_ids=true, to_apply=%region_11.12 | all-reduce | flops 512 | bytes 4096 | tf_op jit(solution)/shard_map/psum | solution.py:37
  280.6 5.8 %all-reduce.7 = (f32[256]{0:T(256)S(1)}, f32[256]{0:T(256)S(1)}) all-reduce(f32[256]{0:T(256)S(1)} %get-tuple-element.11, f32[256]{0:T(256)S(1)} %get-tuple-element.12), channel_id=1, replica_groups=mesh['cluster'=4,'sub_0'=4,'sub_1'=8,'sub_2'=2] {'sub_2'}, use_global_device_ids=true, to_apply=%region_12.13 | all-reduce | flops 512 | bytes 4096 | tf_op jit(solution)/shard_map/psum | solution.py:37
  288.5 22.7 %all_to_all.44 = f32[64,6,256]{2,1,0:T(8,128)S(1)} all-to-all(f32[64,6,256]{2,1,0:T(8,128)S(1)} %broadcast_in_dim.29), channel_id=1, replica_groups=mesh['cluster'=4,'sub_0'=4,'sub_1'=8,'sub_2'=2] {'sub_0','sub_1','sub_2'}, dimensions={0} | all-to-all | bytes 786432 | tf_op jit(solution)/shard_map/all_to_all | solution.py:21
  311.4 23.1 %all_to_all.45 = f32[4,384,256]{2,1,0:T(8,128)S(1)} all-to-all(f32[4,384,256]{2,1,0:T(8,128)S(1)} %broadcast_in_dim.30), channel_id=1, replica_groups=mesh['cluster'=4,'sub_0'=4,'sub_1'=8,'sub_2'=2] {'cluster'}, dimensions={0} | all-to-all | bytes 3145728 | tf_op jit(solution)/shard_map/all_to_all | solution.py:21
  351.8 10.3 %convolution_bitcast_fusion.2 = f32[1024,256]{0,1:T(8,128)} fusion(f32[1024,1024]{1,0:T(8,128)} %param.7, f32[1024,256]{1,0:T(8,128)S(1)} %multiply_subtract_fusion.1, f32[1024,256]{1,0:T(8,128)S(1)} %scatter_fusion.12, f32[1024]{0:T(1024)S(1)} %scatter_fusion), kind=kOutput, calls=%fused_computation.42 | convolution fusion | flops 3221749760 | bytes 7344128 | tf_op jit(solution)/shard_map/dot_general | solution.py:107
  375.9 31.6 %all_to_all.46 = f32[64,6,256]{2,1,0:T(8,128)S(1)} all-to-all(f32[64,6,256]{2,1,0:T(8,128)S(1)} %broadcast_in_dim.31), channel_id=1, replica_groups=mesh['cluster'=4,'sub_0'=4,'sub_1'=8,'sub_2'=2] {'sub_0','sub_1','sub_2'}, dimensions={0} | all-to-all | bytes 786432 | tf_op jit(solution)/shard_map/all_to_all | solution.py:21
  407.7 23.4 %all_to_all.47 = f32[4,384,256]{2,1,0:T(8,128)S(1)} all-to-all(f32[4,384,256]{2,1,0:T(8,128)S(1)} %broadcast_in_dim.32), channel_id=1, replica_groups=mesh['cluster'=4,'sub_0'=4,'sub_1'=8,'sub_2'=2] {'cluster'}, dimensions={0} | all-to-all | bytes 3145728 | tf_op jit(solution)/shard_map/all_to_all | solution.py:21
  446.9 6.9 %psum.176 = f32[256]{0:T(256)S(1)} all-reduce(f32[256]{0:T(256)S(1)} %get-tuple-element.6), channel_id=1, replica_groups=mesh['cluster'=4,'sub_0'=4,'sub_1'=8,'sub_2'=2] {'cluster'}, use_global_device_ids=true, to_apply=%region_27.28 | all-reduce | flops 256 | bytes 2048 | tf_op jit(solution)/shard_map/psum | solution.py:37
  453.8 8.3 %psum.177 = f32[256]{0:T(256)S(1)} all-reduce(f32[256]{0:T(256)S(1)} %psum.176), channel_id=1, replica_groups=mesh['cluster'=4,'sub_0'=4,'sub_1'=8,'sub_2'=2] {'sub_0'}, use_global_device_ids=true, to_apply=%region_28.29 | all-reduce | flops 256 | bytes 2048 | tf_op jit(solution)/shard_map/psum | solution.py:37
  462.1 12.3 %psum.178 = f32[256]{0:T(256)S(1)} all-reduce(f32[256]{0:T(256)S(1)} %psum.177), channel_id=1, replica_groups=mesh['cluster'=4,'sub_0'=4,'sub_1'=8,'sub_2'=2] {'sub_1'}, use_global_device_ids=true, to_apply=%region_29.30 | all-reduce | flops 256 | bytes 2048 | tf_op jit(solution)/shard_map/psum | solution.py:37
  474.4 11.3 %psum.179 = f32[256]{0:T(256)S(1)} all-reduce(f32[256]{0:T(256)S(1)} %psum.178), channel_id=1, replica_groups=mesh['cluster'=4,'sub_0'=4,'sub_1'=8,'sub_2'=2] {'sub_2'}, use_global_device_ids=true, to_apply=%region_30.31 | all-reduce | flops 256 | bytes 2048 | tf_op jit(solution)/shard_map/psum | solution.py:37
  492.1 7.1 %convolution_bitcast_fusion = f32[1024,256]{0,1:T(8,128)S(1)} fusion(f32[1024,256]{1,0:T(8,128)S(1)} %multiply_add_fusion.1, f32[1024,1024]{1,0:T(8,128)S(1)} %copy-done.6), kind=kOutput, calls=%fused_computation.40 | convolution fusion | flops 3221225472 | bytes 6291456 | tf_op jit(solution)/shard_map/dot_general | solution.py:121
  514.5 6.6 %all-reduce.4 = (f32[256]{0:T(256)S(1)}, f32[256]{0:T(256)S(1)}, f32[256]{0:T(256)S(1)}) all-reduce(f32[256]{0:T(256)S(1)} %multiply_reduce_fusion, f32[256]{0:T(256)S(1)} %get-tuple-element.5, f32[256]{0:T(256)S(1)} %get-tuple-element.3), channel_id=1, replica_groups=mesh['cluster'=4,'sub_0'=4,'sub_1'=8,'sub_2'=2] {'cluster'}, use_global_device_ids=true, to_apply=%region_36.37 | all-reduce | flops 768 | bytes 6144 | tf_op jit(solution)/shard_map/psum | solution.py:37
  521.1 6.5 %all-reduce.2 = (f32[256]{0:T(256)S(1)}, f32[256]{0:T(256)S(1)}, f32[256]{0:T(256)S(1)}) all-reduce(f32[256]{0:T(256)S(1)} %get-tuple-element.18, f32[256]{0:T(256)S(1)} %get-tuple-element.19, f32[256]{0:T(256)S(1)} %get-tuple-element.20), channel_id=1, replica_groups=mesh['cluster'=4,'sub_0'=4,'sub_1'=8,'sub_2'=2] {'sub_0'}, use_global_device_ids=true, to_apply=%region_37.38 | all-reduce | flops 768 | bytes 6144 | tf_op jit(solution)/shard_map/psum | solution.py:37
  527.6 17.9 %all-reduce = (f32[256]{0:T(256)S(1)}, f32[256]{0:T(256)S(1)}, f32[256]{0:T(256)S(1)}) all-reduce(f32[256]{0:T(256)S(1)} %get-tuple-element.13, f32[256]{0:T(256)S(1)} %get-tuple-element.14, f32[256]{0:T(256)S(1)} %get-tuple-element.15), channel_id=1, replica_groups=mesh['cluster'=4,'sub_0'=4,'sub_1'=8,'sub_2'=2] {'sub_1'}, use_global_device_ids=true, to_apply=%region_38.39 | all-reduce | flops 768 | bytes 6144 | tf_op jit(solution)/shard_map/psum | solution.py:37
  (143 shorter events, 180.6 us)
Async XLA Ops:
  0.6 70.1 %copy-start = (f32[6,1536]{1,0:T(8,128)S(1)}, f32[6,1536]{1,0:T(8,128)}, u32[]{:S(2)}) copy-start(f32[6,1536]{1,0:T(8,128)} %param.9) | copy-start | bytes 110596
  2.7 7.6 %collective-permute-start = (f32[128,256]{1,0:T(8,128)S(1)}, f32[128,256]{1,0:T(8,128)S(1)}, u32[]{:S(2)}, u32[]{:S(2)}) collective-permute-start(f32[128,256]{1,0:T(8,128)S(1)} %gather_fusion), channel_id=1, source_target_pairs={{0,1},{1,2},{2,3},{3,4},{4,5},{5,6},{6,7},{7,8},{8,9},{9,10},{10,1... | collective-permute-start | bytes 393224 | tf_op jit(solution)/shard_map/ppermute | solution.py:16
  8.4 6.3 %collective-permute-start.1 = (f32[128,256]{1,0:T(8,128)S(1)}, f32[128,256]{1,0:T(8,128)S(1)}, u32[]{:S(2)}, u32[]{:S(2)}) collective-permute-start(f32[128,256]{1,0:T(8,128)S(1)} %gather_fusion.1), channel_id=1, source_target_pairs={{1,0},{2,1},{3,2},{4,3},{5,4},{6,5},{7,6},{8,7},{9,8},{10,9},{11,1... | collective-permute-start | bytes 393224 | tf_op jit(solution)/shard_map/ppermute | solution.py:16
  12.0 4.3 copy-start.8
  75.4 8.8 %collective-permute-start.2 = (f32[128,256]{1,0:T(8,128)S(1)}, f32[128,256]{1,0:T(8,128)S(1)}, u32[]{:S(2)}, u32[]{:S(2)}) collective-permute-start(f32[128,256]{1,0:T(8,128)S(1)} %gather_fusion.2), channel_id=1, source_target_pairs={{0,1},{1,2},{2,3},{3,4},{4,5},{5,6},{6,7},{7,8},{8,9},{9,10},{10,1... | collective-permute-start | bytes 393224 | tf_op jit(solution)/shard_map/ppermute | solution.py:16
  80.2 6.3 %collective-permute-start.3 = (f32[128,256]{1,0:T(8,128)S(1)}, f32[128,256]{1,0:T(8,128)S(1)}, u32[]{:S(2)}, u32[]{:S(2)}) collective-permute-start(f32[128,256]{1,0:T(8,128)S(1)} %gather_fusion.3), channel_id=1, source_target_pairs={{1,0},{2,1},{3,2},{4,3},{5,4},{6,5},{7,6},{8,7},{9,8},{10,9},{11,1... | collective-permute-start | bytes 393224 | tf_op jit(solution)/shard_map/ppermute | solution.py:16
  112.8 6.4 %collective-permute-start.4 = (f32[128,256]{1,0:T(8,128)}, f32[128,256]{1,0:T(8,128)S(1)}, u32[]{:S(2)}, u32[]{:S(2)}) collective-permute-start(f32[128,256]{1,0:T(8,128)} %gather_fusion.4), channel_id=1, source_target_pairs={{0,1},{1,2},{2,3},{3,4},{4,5},{5,6},{6,7},{7,8},{8,9},{9,10},{10,1... | collective-permute-start | bytes 393224 | tf_op jit(solution)/shard_map/ppermute | solution.py:16
  117.3 6.5 %collective-permute-start.5 = (f32[128,256]{1,0:T(8,128)}, f32[128,256]{1,0:T(8,128)S(1)}, u32[]{:S(2)}, u32[]{:S(2)}) collective-permute-start(f32[128,256]{1,0:T(8,128)} %gather_fusion.5), channel_id=1, source_target_pairs={{1,0},{2,1},{3,2},{4,3},{5,4},{6,5},{7,6},{8,7},{9,8},{10,9},{11,1... | collective-permute-start | bytes 393224 | tf_op jit(solution)/shard_map/ppermute | solution.py:16
  193.7 8.6 %collective-permute-start.6 = (f32[128,256]{1,0:T(8,128)}, f32[128,256]{1,0:T(8,128)S(1)}, u32[]{:S(2)}, u32[]{:S(2)}) collective-permute-start(f32[128,256]{1,0:T(8,128)} %gather_fusion.6), channel_id=1, source_target_pairs={{0,1},{1,2},{2,3},{3,4},{4,5},{5,6},{6,7},{7,8},{8,9},{9,10},{10,1... | collective-permute-start | bytes 393224 | tf_op jit(solution)/shard_map/ppermute | solution.py:16
  200.4 6.5 %collective-permute-start.7 = (f32[128,256]{1,0:T(8,128)}, f32[128,256]{1,0:T(8,128)S(1)}, u32[]{:S(2)}, u32[]{:S(2)}) collective-permute-start(f32[128,256]{1,0:T(8,128)} %gather_fusion.7), channel_id=1, source_target_pairs={{1,0},{2,1},{3,2},{4,3},{5,4},{6,5},{7,6},{8,7},{9,8},{10,9},{11,1... | collective-permute-start | bytes 393224 | tf_op jit(solution)/shard_map/ppermute | solution.py:16
  228.5 7.0 %collective-permute-start.8 = (f32[128,256]{1,0:T(8,128)}, f32[128,256]{1,0:T(8,128)S(1)}, u32[]{:S(2)}, u32[]{:S(2)}) collective-permute-start(f32[128,256]{1,0:T(8,128)} %gather_fusion.8), channel_id=1, source_target_pairs={{0,1},{1,2},{2,3},{3,4},{4,5},{5,6},{6,7},{7,8},{8,9},{9,10},{10,1... | collective-permute-start | bytes 393224 | tf_op jit(solution)/shard_map/ppermute | solution.py:16
  233.5 6.5 %collective-permute-start.9 = (f32[128,256]{1,0:T(8,128)}, f32[128,256]{1,0:T(8,128)S(1)}, u32[]{:S(2)}, u32[]{:S(2)}) collective-permute-start(f32[128,256]{1,0:T(8,128)} %gather_fusion.9), channel_id=1, source_target_pairs={{1,0},{2,1},{3,2},{4,3},{5,4},{6,5},{7,6},{8,7},{9,8},{10,9},{11,1... | collective-permute-start | bytes 393224 | tf_op jit(solution)/shard_map/ppermute | solution.py:16
  287.9 64.0 %copy-start.1 = (f32[1024,256]{1,0:T(8,128)}, f32[1024,256]{1,0:T(8,128)S(1)}, u32[]{:S(2)}) copy-start(f32[1024,256]{1,0:T(8,128)S(1)} %multiply_subtract_fusion.1) | copy-start | bytes 3145732
  339.2 6.5 %collective-permute-start.10 = (f32[128,256]{1,0:T(8,128)S(1)}, f32[128,256]{1,0:T(8,128)S(1)}, u32[]{:S(2)}, u32[]{:S(2)}) collective-permute-start(f32[128,256]{1,0:T(8,128)S(1)} %gather_fusion.10), channel_id=1, source_target_pairs={{0,1},{1,2},{2,3},{3,4},{4,5},{5,6},{6,7},{7,8},{8,9},{9,10},{10,1... | collective-permute-start | bytes 393224 | tf_op jit(solution)/shard_map/ppermute | solution.py:16
  343.8 6.3 %collective-permute-start.11 = (f32[128,256]{1,0:T(8,128)S(1)}, f32[128,256]{1,0:T(8,128)S(1)}, u32[]{:S(2)}, u32[]{:S(2)}) collective-permute-start(f32[128,256]{1,0:T(8,128)S(1)} %gather_fusion.11), channel_id=1, source_target_pairs={{1,0},{2,1},{3,2},{4,3},{5,4},{6,5},{7,6},{8,7},{9,8},{10,9},{11,1... | collective-permute-start | bytes 393224 | tf_op jit(solution)/shard_map/ppermute | solution.py:16
  364.5 5.1 collective-permute-start.12
  367.1 6.3 %collective-permute-start.13 = (f32[128,256]{1,0:T(8,128)S(1)}, f32[128,256]{1,0:T(8,128)S(1)}, u32[]{:S(2)}, u32[]{:S(2)}) collective-permute-start(f32[128,256]{1,0:T(8,128)S(1)} %gather_fusion.13), channel_id=1, source_target_pairs={{1,0},{2,1},{3,2},{4,3},{5,4},{6,5},{7,6},{8,7},{9,8},{10,9},{11,1... | collective-permute-start | bytes 393224 | tf_op jit(solution)/shard_map/ppermute | solution.py:16
  439.3 46.5 %collective-permute-start.14 = (f32[128,256]{1,0:T(8,128)}, f32[128,256]{1,0:T(8,128)}, u32[]{:S(2)}, u32[]{:S(2)}) collective-permute-start(f32[128,256]{1,0:T(8,128)} %gather_fusion.14), channel_id=1, source_target_pairs={{0,1},{1,2},{2,3},{3,4},{4,5},{5,6},{6,7},{7,8},{8,9},{9,10},{10,1... | collective-permute-start | bytes 393224 | tf_op jit(solution)/shard_map/ppermute | solution.py:16
  443.4 44.5 %collective-permute-start.15 = (f32[128,256]{1,0:T(8,128)S(1)}, f32[128,256]{1,0:T(8,128)S(1)}, u32[]{:S(2)}, u32[]{:S(2)}) collective-permute-start(f32[128,256]{1,0:T(8,128)S(1)} %gather_fusion.15), channel_id=1, source_target_pairs={{1,0},{2,1},{3,2},{4,3},{5,4},{6,5},{7,6},{8,7},{9,8},{10,9},{11,1... | collective-permute-start | bytes 393224 | tf_op jit(solution)/shard_map/ppermute | solution.py:16
  489.6 2.6 copy-start.6
  500.3 6.6 %collective-permute-start.16 = (f32[128,256]{1,0:T(8,128)S(1)}, f32[128,256]{1,0:T(8,128)S(1)}, u32[]{:S(2)}, u32[]{:S(2)}) collective-permute-start(f32[128,256]{1,0:T(8,128)S(1)} %gather_fusion.16), channel_id=1, source_target_pairs={{0,1},{1,2},{2,3},{3,4},{4,5},{5,6},{6,7},{7,8},{8,9},{9,10},{10,1... | collective-permute-start | bytes 393224 | tf_op jit(solution)/shard_map/ppermute | solution.py:16
  504.9 6.3 %collective-permute-start.17 = (f32[128,256]{1,0:T(8,128)S(1)}, f32[128,256]{1,0:T(8,128)S(1)}, u32[]{:S(2)}, u32[]{:S(2)}) collective-permute-start(f32[128,256]{1,0:T(8,128)S(1)} %gather_fusion.17), channel_id=1, source_target_pairs={{1,0},{2,1},{3,2},{4,3},{5,4},{6,5},{7,6},{8,7},{9,8},{10,9},{11,1... | collective-permute-start | bytes 393224 | tf_op jit(solution)/shard_map/ppermute | solution.py:16
  512.9 36.7 %copy-start.2 = (f32[1024,256]{1,0:T(8,128)S(1)}, f32[1024,256]{1,0:T(8,128)}, u32[]{:S(2)}) copy-start(f32[1024,256]{1,0:T(8,128)} %copy-done.1) | copy-start | bytes 3145732
  512.9 36.7 %copy-start.5 = (f32[1024,256]{1,0:T(8,128)S(1)}, f32[1024,256]{1,0:T(8,128)}, u32[]{:S(2)}) copy-start(f32[1024,256]{1,0:T(8,128)} %copy-done.3) | copy-start | bytes 3145732
  (4 other events, 4.9 us)
where the time goes:
time: 563 us; the launch traced here: 553 us
  blocking collectives  324 us (58%)
  other arithmetic  60.8 us (11%)
  matrix products  56.8 us (10%)
  starting transfers between devices  49.9 us (9%)
  local copies, waits for them, and re-layouts  43.9 us (8%)
  waiting for transfers between devices  16.1 us (3%)
    all_to_all x8, blocking collectives, from_everyone(): return lax.all_to_all(copies, axis, split_axis=0, concat_axis=0, tiled=True)  209 us
    psum x12, blocking collectives, by_axis(): array = lax.psum(array, axis)  115 us
    ppermute x18, starting transfers between devices, passed_along(): lax.ppermute(value, axis, [(source, source + steps) for source in range(i...  49.9 us
    scatter-add x8, other arithmetic, gather_onto_subdomain_vector(): return back_rows.at[left_neighbour_rows].add(from_left).at[right_neighbou...  28.9 us
    dot_general x2, matrix products, shards(): jnp.dot(boundary_solve_blocks, interface_weights * projected_residual, pr...  20.6 us
    scatter-add x10, other arithmetic, assemble_dual(): return deformation_vector.at[left_neighbour_rows].add(from_left).at[right...  20.1 us
    dot_general x2, matrix products, shards(): jnp.dot(dual_ops, search_direction, precision=finest_tier, preferred_elem...  17.3 us
    ppermute x18, waiting for transfers between devices, passed_along(): lax.ppermute(value, axis, [(source, source + steps) for source in range(i...  16.1 us
  transfers between devices with their start and end apart: 18, of which 8 were waited for; matrix products, arithmetic and copies ran while one was open for 6% of the time, Pallas kernels for 0%

commit v1 on v0

--- a/solution.py
+++ b/solution.py
@@ -3,6 +3,7 @@
 from jax import lax
 from jax.sharding import Mesh
 from jax.sharding import PartitionSpec as P
+from jax.lax import all_gather
 
 ITERS = 2
 CLUSTER_SUB = ("cluster", "sub_0", "sub_1", "sub_2")
@@ -34,7 +35,10 @@
 
 def by_axis(array, axes):
     for axis in axes:
-        array = lax.psum(array, axis)
+        apply_sums_all_now = lambda my_tile, mesh_dim: jnp.sum(
+            all_gather(my_tile, axis_name=mesh_dim), axis=0
+        )
+        array = apply_sums_all_now(array, axis)
     return array
 
 

time: 563 us -> 632 us (1.12)
  blocking collectives: 324 us -> 414 us
  other arithmetic: 60.8 us -> 50 us
  matrix products: 56.8 us -> 50.2 us
    all_gather x0 -> x24, blocking collectives: none -> 205 us  [by_axis(): all_gather(my_tile, axis_name=mesh_dim)]
    psum x12 -> x0, blocking collectives: 115 us -> none  [by_axis(): array = lax.psum(array, axis)]
    scatter-add x8, other arithmetic: 28.9 us -> 17.5 us  [gather_onto_subdomain_vector(): return back_rows.at[left_neighbour_rows].add(from_left).at[right_neighbou...]
    dot_general x4, matrix products: 10.4 us -> 3.48 us  [coarse_fold(): jnp.dot(coarse_rows, piece, precision=finest_tier, preferred_element_type...]
  transfers between devices with their start and end apart: 18 -> 18, of which waited for: 8 -> 7; matrix products, arithmetic and copies ran while one was open for 6% -> 5% of each run, Pallas kernels for 0% -> 0%
where the time goes in v1:
time: 632 us; the launch traced here: 624 us
  blocking collectives  414 us (66%)
  starting transfers between devices  50.3 us (8%)
  matrix products  50.2 us (8%)
  other arithmetic  50 us (8%)
  local copies, waits for them, and re-layouts  43.9 us (7%)
  waiting for transfers between devices  13.3 us (2%)
    all_to_all x8, blocking collectives, from_everyone(): return lax.all_to_all(copies, axis, split_axis=0, concat_axis=0, tiled=True)  209 us
    all_gather x24, blocking collectives, by_axis(): all_gather(my_tile, axis_name=mesh_dim)  205 us
    ppermute x18, starting transfers between devices, passed_along(): lax.ppermute(value, axis, [(source, source + steps) for source in range(i...  50.3 us
    dot_general x2, matrix products, shards(): jnp.dot(boundary_solve_blocks, interface_weights * projected_residual, pr...  20.6 us
    scatter-add x10, other arithmetic, assemble_dual(): return deformation_vector.at[left_neighbour_rows].add(from_left).at[right...  20.1 us
    scatter-add x8, other arithmetic, gather_onto_subdomain_vector(): return back_rows.at[left_neighbour_rows].add(from_left).at[right_neighbou...  17.5 us
    dot_general x2, matrix products, shards(): jnp.dot(dual_ops, search_direction, precision=finest_tier, preferred_elem...  17.3 us
    ppermute x18, waiting for transfers between devices, passed_along(): lax.ppermute(value, axis, [(source, source + steps) for source in range(i...  13.3 us
  transfers between devices with their start and end apart: 18, of which 7 were waited for; matrix products, arithmetic and copies ran while one was open for 5% of the time, Pallas kernels for 0%

profile of v1, /device:TPU:1, one launch (start us, length us, event | category | flops | bytes accessed | tf_op | source)
XLA Modules:
  0.0 623.8 jit_solution(14258714310578211915)
XLA Ops:
  17.0 29.4 %all_to_all.40 = f32[64,6,256]{2,1,0:T(8,128)S(1)} all-to-all(f32[64,6,256]{2,1,0:T(8,128)S(1)} %broadcast_in_dim.25), channel_id=1, replica_groups=mesh['cluster'=4,'sub_0'=4,'sub_1'=8,'sub_2'=2] {'sub_0','sub_1','sub_2'}, dimensions={0} | all-to-all | bytes 786432 | tf_op jit(solution)/shard_map/all_to_all | solution.py:22
  46.6 24.1 %all_to_all.41 = f32[4,384,256]{2,1,0:T(8,128)S(1)} all-to-all(f32[4,384,256]{2,1,0:T(8,128)S(1)} %broadcast_in_dim.26), channel_id=1, replica_groups=mesh['cluster'=4,'sub_0'=4,'sub_1'=8,'sub_2'=2] {'cluster'}, dimensions={0} | all-to-all | bytes 3145728 | tf_op jit(solution)/shard_map/all_to_all | solution.py:22
  86.7 10.3 %convolution_bitcast_fusion.6 = f32[1024,256]{0,1:T(8,128)} fusion(f32[1024,1024]{1,0:T(8,128)} %param.7, f32[1024,256]{1,0:T(8,128)S(1)} %scatter_fusion.2, f32[1024,256]{1,0:T(8,128)S(1)} %scatter_fusion.4, f32[1024]{0:T(1024)S(1)} %scatter_fusion), kind=kOutput, calls=%fused_computation.46 | convolution fusion | flops 3221749760 | bytes 7344128 | tf_op jit(solution)/shard_map/dot_general | solution.py:111
  113.4 31.7 %all_to_all.42 = f32[64,6,256]{2,1,0:T(8,128)} all-to-all(f32[64,6,256]{2,1,0:T(8,128)S(1)} %broadcast_in_dim.27), channel_id=1, replica_groups=mesh['cluster'=4,'sub_0'=4,'sub_1'=8,'sub_2'=2] {'sub_0','sub_1','sub_2'}, dimensions={0} | all-to-all | bytes 786432 | tf_op jit(solution)/shard_map/all_to_all | solution.py:22
  148.1 23.6 %all_to_all.43 = f32[4,384,256]{2,1,0:T(8,128)S(1)} all-to-all(f32[4,384,256]{2,1,0:T(8,128)S(1)} %broadcast_in_dim.28), channel_id=1, replica_groups=mesh['cluster'=4,'sub_0'=4,'sub_1'=8,'sub_2'=2] {'cluster'}, dimensions={0} | all-to-all | bytes 3145728 | tf_op jit(solution)/shard_map/all_to_all | solution.py:22
  198.6 10.3 %convolution_bitcast_fusion.4 = f32[1024,256]{0,1:T(8,128)} fusion(f32[1024,256]{1,0:T(8,128)S(1)} %multiply_subtract_fusion.2, f32[1024,1024]{1,0:T(8,128)} %param.6), kind=kOutput, calls=%fused_computation.44 | convolution fusion | flops 3221225472 | bytes 6291456 | tf_op jit(solution)/shard_map/dot_general | solution.py:125
  230.9 8.5 %all-gather.24 = f32[4,1,256]{2,1,0:T(1,128)S(1)} all-gather(f32[1,1,256]{2,1,0:T(1,128)S(1)} %bitcast.99), channel_id=2, replica_groups=mesh['cluster'=4,'sub_0'=4,'sub_1'=8,'sub_2'=2] {'cluster'}, dimensions={0}, use_global_device_ids=true | all-gather | bytes 5120 | tf_op jit(solution)/shard_map/all_gather | solution.py:39
  257.0 18.9 %all-gather.30 = f32[8,1,256]{2,1,0:T(1,128)S(1)} all-gather(f32[1,1,256]{2,1,0:T(1,128)S(1)} %bitcast.113), channel_id=8, replica_groups=mesh['cluster'=4,'sub_0'=4,'sub_1'=8,'sub_2'=2] {'sub_1'}, dimensions={0}, use_global_device_ids=true | all-gather | bytes 9216 | tf_op jit(solution)/shard_map/all_gather | solution.py:39
  275.9 9.4 %all-gather.31 = f32[2,1,256]{2,1,0:T(1,128)S(1)} all-gather(f32[1,1,256]{2,1,0:T(1,128)S(1)} %bitcast.102), channel_id=9, replica_groups=mesh['cluster'=4,'sub_0'=4,'sub_1'=8,'sub_2'=2] {'sub_2'}, dimensions={0}, use_global_device_ids=true | all-gather | bytes 3072 | tf_op jit(solution)/shard_map/all_gather | solution.py:39
  285.3 11.7 %all-gather.26 = f32[8,1,256]{2,1,0:T(1,128)S(1)} all-gather(f32[1,1,256]{2,1,0:T(1,128)S(1)} %bitcast.109), channel_id=4, replica_groups=mesh['cluster'=4,'sub_0'=4,'sub_1'=8,'sub_2'=2] {'sub_1'}, dimensions={0}, use_global_device_ids=true | all-gather | bytes 9216 | tf_op jit(solution)/shard_map/all_gather | solution.py:39
  304.6 21.9 %all_to_all.44 = f32[64,6,256]{2,1,0:T(8,128)S(1)} all-to-all(f32[64,6,256]{2,1,0:T(8,128)S(1)} %broadcast_in_dim.29), channel_id=1, replica_groups=mesh['cluster'=4,'sub_0'=4,'sub_1'=8,'sub_2'=2] {'sub_0','sub_1','sub_2'}, dimensions={0} | all-to-all | bytes 786432 | tf_op jit(solution)/shard_map/all_to_all | solution.py:22
  326.7 23.1 %all_to_all.45 = f32[4,384,256]{2,1,0:T(8,128)S(1)} all-to-all(f32[4,384,256]{2,1,0:T(8,128)S(1)} %broadcast_in_dim.30), channel_id=1, replica_groups=mesh['cluster'=4,'sub_0'=4,'sub_1'=8,'sub_2'=2] {'cluster'}, dimensions={0} | all-to-all | bytes 3145728 | tf_op jit(solution)/shard_map/all_to_all | solution.py:22
  365.8 10.3 %convolution_bitcast_fusion.2 = f32[1024,256]{0,1:T(8,128)} fusion(f32[1024,1024]{1,0:T(8,128)} %param.7, f32[1024,256]{1,0:T(8,128)S(1)} %multiply_subtract_fusion.1, f32[1024,256]{1,0:T(8,128)S(1)} %scatter_fusion.12, f32[1024]{0:T(1024)S(1)} %scatter_fusion), kind=kOutput, calls=%fused_computation.42 | convolution fusion | flops 3221749760 | bytes 7344128 | tf_op jit(solution)/shard_map/dot_general | solution.py:111
  389.9 31.6 %all_to_all.46 = f32[64,6,256]{2,1,0:T(8,128)S(1)} all-to-all(f32[64,6,256]{2,1,0:T(8,128)S(1)} %broadcast_in_dim.31), channel_id=1, replica_groups=mesh['cluster'=4,'sub_0'=4,'sub_1'=8,'sub_2'=2] {'sub_0','sub_1','sub_2'}, dimensions={0} | all-to-all | bytes 786432 | tf_op jit(solution)/shard_map/all_to_all | solution.py:22
  421.7 23.4 %all_to_all.47 = f32[4,384,256]{2,1,0:T(8,128)S(1)} all-to-all(f32[4,384,256]{2,1,0:T(8,128)S(1)} %broadcast_in_dim.32), channel_id=1, replica_groups=mesh['cluster'=4,'sub_0'=4,'sub_1'=8,'sub_2'=2] {'cluster'}, dimensions={0} | all-to-all | bytes 3145728 | tf_op jit(solution)/shard_map/all_to_all | solution.py:22
  465.5 7.3 %all-gather.33 = f32[4,1,256]{2,1,0:T(1,128)S(1)} all-gather(f32[1,1,256]{2,1,0:T(1,128)S(1)} %bitcast.114), channel_id=11, replica_groups=mesh['cluster'=4,'sub_0'=4,'sub_1'=8,'sub_2'=2] {'sub_0'}, dimensions={0}, use_global_device_ids=true | all-gather | bytes 5120 | tf_op jit(solution)/shard_map/all_gather | solution.py:39
  472.8 11.9 %all-gather.34 = f32[8,1,256]{2,1,0:T(1,128)S(1)} all-gather(f32[1,1,256]{2,1,0:T(1,128)S(1)} %bitcast.115), channel_id=12, replica_groups=mesh['cluster'=4,'sub_0'=4,'sub_1'=8,'sub_2'=2] {'sub_1'}, dimensions={0}, use_global_device_ids=true | all-gather | bytes 9216 | tf_op jit(solution)/shard_map/all_gather | solution.py:39
  484.7 10.6 %all-gather.35 = f32[2,1,256]{2,1,0:T(1,128)S(1)} all-gather(f32[1,1,256]{2,1,0:T(1,128)S(1)} %bitcast.104), channel_id=13, replica_groups=mesh['cluster'=4,'sub_0'=4,'sub_1'=8,'sub_2'=2] {'sub_2'}, dimensions={0}, use_global_device_ids=true | all-gather | bytes 3072 | tf_op jit(solution)/shard_map/all_gather | solution.py:39
  527.9 12.8 %all-gather.42 = f32[8,1,256]{2,1,0:T(1,128)S(1)} all-gather(f32[1,1,256]{2,1,0:T(1,128)S(1)} %bitcast.117), channel_id=20, replica_groups=mesh['cluster'=4,'sub_0'=4,'sub_1'=8,'sub_2'=2] {'sub_1'}, dimensions={0}, use_global_device_ids=true | all-gather | bytes 9216 | tf_op jit(solution)/shard_map/all_gather | solution.py:39
  540.7 9.7 %all-gather.43 = f32[2,1,256]{2,1,0:T(1,128)S(1)} all-gather(f32[1,1,256]{2,1,0:T(1,128)S(1)} %bitcast.105), channel_id=21, replica_groups=mesh['cluster'=4,'sub_0'=4,'sub_1'=8,'sub_2'=2] {'sub_2'}, dimensions={0}, use_global_device_ids=true | all-gather | bytes 3072 | tf_op jit(solution)/shard_map/all_gather | solution.py:39
  563.1 11.6 %all-gather.46 = f32[8,1,256]{2,1,0:T(1,128)S(1)} all-gather(f32[1,1,256]{2,1,0:T(1,128)S(1)} %bitcast.119), channel_id=24, replica_groups=mesh['cluster'=4,'sub_0'=4,'sub_1'=8,'sub_2'=2] {'sub_1'}, dimensions={0}, use_global_device_ids=true | all-gather | bytes 9216 | tf_op jit(solution)/shard_map/all_gather | solution.py:39
  574.7 8.9 %all-gather.47 = f32[2,1,256]{2,1,0:T(1,128)S(1)} all-gather(f32[1,1,256]{2,1,0:T(1,128)S(1)} %bitcast.106), channel_id=25, replica_groups=mesh['cluster'=4,'sub_0'=4,'sub_1'=8,'sub_2'=2] {'sub_2'}, dimensions={0}, use_global_device_ids=true | all-gather | bytes 3072 | tf_op jit(solution)/shard_map/all_gather | solution.py:39
  601.5 9.9 %all-gather.38 = f32[8,1,256]{2,1,0:T(1,128)S(1)} all-gather(f32[1,1,256]{2,1,0:T(1,128)S(1)} %bitcast.121), channel_id=16, replica_groups=mesh['cluster'=4,'sub_0'=4,'sub_1'=8,'sub_2'=2] {'sub_1'}, dimensions={0}, use_global_device_ids=true | all-gather | bytes 9216 | tf_op jit(solution)/shard_map/all_gather | solution.py:39
  611.4 9.0 %all-gather.39 = f32[2,1,256]{2,1,0:T(1,128)S(1)} all-gather(f32[1,1,256]{2,1,0:T(1,128)S(1)} %bitcast.107), channel_id=17, replica_groups=mesh['cluster'=4,'sub_0'=4,'sub_1'=8,'sub_2'=2] {'sub_2'}, dimensions={0}, use_global_device_ids=true | all-gather | bytes 3072 | tf_op jit(solution)/shard_map/all_gather | solution.py:39
  (179 shorter events, 242.1 us)
Async XLA Ops:
  0.6 70.1 %copy-start = (f32[6,1536]{1,0:T(8,128)S(1)}, f32[6,1536]{1,0:T(8,128)}, u32[]{:S(2)}) copy-start(f32[6,1536]{1,0:T(8,128)} %param.9) | copy-start | bytes 110596
  2.7 7.6 %collective-permute-start = (f32[128,256]{1,0:T(8,128)S(1)}, f32[128,256]{1,0:T(8,128)S(1)}, u32[]{:S(2)}, u32[]{:S(2)}) collective-permute-start(f32[128,256]{1,0:T(8,128)S(1)} %gather_fusion), channel_id=1, source_target_pairs={{0,1},{1,2},{2,3},{3,4},{4,5},{5,6},{6,7},{7,8},{8,9},{9,10},{10,1... | collective-permute-start | bytes 393224 | tf_op jit(solution)/shard_map/ppermute | solution.py:17
  8.4 6.3 %collective-permute-start.1 = (f32[128,256]{1,0:T(8,128)S(1)}, f32[128,256]{1,0:T(8,128)S(1)}, u32[]{:S(2)}, u32[]{:S(2)}) collective-permute-start(f32[128,256]{1,0:T(8,128)S(1)} %gather_fusion.1), channel_id=1, source_target_pairs={{1,0},{2,1},{3,2},{4,3},{5,4},{6,5},{7,6},{8,7},{9,8},{10,9},{11,1... | collective-permute-start | bytes 393224 | tf_op jit(solution)/shard_map/ppermute | solution.py:17
  12.0 4.3 copy-start.8
  73.7 8.8 %collective-permute-start.2 = (f32[128,256]{1,0:T(8,128)S(1)}, f32[128,256]{1,0:T(8,128)S(1)}, u32[]{:S(2)}, u32[]{:S(2)}) collective-permute-start(f32[128,256]{1,0:T(8,128)S(1)} %gather_fusion.2), channel_id=1, source_target_pairs={{0,1},{1,2},{2,3},{3,4},{4,5},{5,6},{6,7},{7,8},{8,9},{9,10},{10,1... | collective-permute-start | bytes 393224 | tf_op jit(solution)/shard_map/ppermute | solution.py:17
  78.6 6.3 %collective-permute-start.3 = (f32[128,256]{1,0:T(8,128)S(1)}, f32[128,256]{1,0:T(8,128)S(1)}, u32[]{:S(2)}, u32[]{:S(2)}) collective-permute-start(f32[128,256]{1,0:T(8,128)S(1)} %gather_fusion.3), channel_id=1, source_target_pairs={{1,0},{2,1},{3,2},{4,3},{5,4},{6,5},{7,6},{8,7},{9,8},{10,9},{11,1... | collective-permute-start | bytes 393224 | tf_op jit(solution)/shard_map/ppermute | solution.py:17
  100.0 6.4 %collective-permute-start.4 = (f32[128,256]{1,0:T(8,128)}, f32[128,256]{1,0:T(8,128)S(1)}, u32[]{:S(2)}, u32[]{:S(2)}) collective-permute-start(f32[128,256]{1,0:T(8,128)} %gather_fusion.4), channel_id=1, source_target_pairs={{0,1},{1,2},{2,3},{3,4},{4,5},{5,6},{6,7},{7,8},{8,9},{9,10},{10,1... | collective-permute-start | bytes 393224 | tf_op jit(solution)/shard_map/ppermute | solution.py:17
  104.4 6.5 %collective-permute-start.5 = (f32[128,256]{1,0:T(8,128)}, f32[128,256]{1,0:T(8,128)S(1)}, u32[]{:S(2)}, u32[]{:S(2)}) collective-permute-start(f32[128,256]{1,0:T(8,128)} %gather_fusion.5), channel_id=1, source_target_pairs={{1,0},{2,1},{3,2},{4,3},{5,4},{6,5},{7,6},{8,7},{9,8},{10,9},{11,1... | collective-permute-start | bytes 393224 | tf_op jit(solution)/shard_map/ppermute | solution.py:17
  179.7 8.6 %collective-permute-start.6 = (f32[128,256]{1,0:T(8,128)}, f32[128,256]{1,0:T(8,128)S(1)}, u32[]{:S(2)}, u32[]{:S(2)}) collective-permute-start(f32[128,256]{1,0:T(8,128)} %gather_fusion.6), channel_id=1, source_target_pairs={{0,1},{1,2},{2,3},{3,4},{4,5},{5,6},{6,7},{7,8},{8,9},{9,10},{10,1... | collective-permute-start | bytes 393224 | tf_op jit(solution)/shard_map/ppermute | solution.py:17
  186.3 6.5 %collective-permute-start.7 = (f32[128,256]{1,0:T(8,128)}, f32[128,256]{1,0:T(8,128)S(1)}, u32[]{:S(2)}, u32[]{:S(2)}) collective-permute-start(f32[128,256]{1,0:T(8,128)} %gather_fusion.7), channel_id=1, source_target_pairs={{1,0},{2,1},{3,2},{4,3},{5,4},{6,5},{7,6},{8,7},{9,8},{10,9},{11,1... | collective-permute-start | bytes 393224 | tf_op jit(solution)/shard_map/ppermute | solution.py:17
  214.0 7.1 %collective-permute-start.8 = (f32[128,256]{1,0:T(8,128)}, f32[128,256]{1,0:T(8,128)S(1)}, u32[]{:S(2)}, u32[]{:S(2)}) collective-permute-start(f32[128,256]{1,0:T(8,128)} %gather_fusion.8), channel_id=1, source_target_pairs={{0,1},{1,2},{2,3},{3,4},{4,5},{5,6},{6,7},{7,8},{8,9},{9,10},{10,1... | collective-permute-start | bytes 393224 | tf_op jit(solution)/shard_map/ppermute | solution.py:17
  219.1 6.5 %collective-permute-start.9 = (f32[128,256]{1,0:T(8,128)}, f32[128,256]{1,0:T(8,128)S(1)}, u32[]{:S(2)}, u32[]{:S(2)}) collective-permute-start(f32[128,256]{1,0:T(8,128)} %gather_fusion.9), channel_id=1, source_target_pairs={{1,0},{2,1},{3,2},{4,3},{5,4},{6,5},{7,6},{8,7},{9,8},{10,9},{11,1... | collective-permute-start | bytes 393224 | tf_op jit(solution)/shard_map/ppermute | solution.py:17
  303.9 61.9 %copy-start.1 = (f32[1024,256]{1,0:T(8,128)}, f32[1024,256]{1,0:T(8,128)S(1)}, u32[]{:S(2)}) copy-start(f32[1024,256]{1,0:T(8,128)S(1)} %multiply_subtract_fusion.1) | copy-start | bytes 3145732
  352.8 6.8 %collective-permute-start.10 = (f32[128,256]{1,0:T(8,128)S(1)}, f32[128,256]{1,0:T(8,128)S(1)}, u32[]{:S(2)}, u32[]{:S(2)}) collective-permute-start(f32[128,256]{1,0:T(8,128)S(1)} %gather_fusion.10), channel_id=1, source_target_pairs={{0,1},{1,2},{2,3},{3,4},{4,5},{5,6},{6,7},{7,8},{8,9},{9,10},{10,1... | collective-permute-start | bytes 393224 | tf_op jit(solution)/shard_map/ppermute | solution.py:17
  357.6 6.3 %collective-permute-start.11 = (f32[128,256]{1,0:T(8,128)S(1)}, f32[128,256]{1,0:T(8,128)S(1)}, u32[]{:S(2)}, u32[]{:S(2)}) collective-permute-start(f32[128,256]{1,0:T(8,128)S(1)} %gather_fusion.11), channel_id=1, source_target_pairs={{1,0},{2,1},{3,2},{4,3},{5,4},{6,5},{7,6},{8,7},{9,8},{10,9},{11,1... | collective-permute-start | bytes 393224 | tf_op jit(solution)/shard_map/ppermute | solution.py:17
  378.5 5.1 collective-permute-start.12
  381.1 6.3 %collective-permute-start.13 = (f32[128,256]{1,0:T(8,128)S(1)}, f32[128,256]{1,0:T(8,128)S(1)}, u32[]{:S(2)}, u32[]{:S(2)}) collective-permute-start(f32[128,256]{1,0:T(8,128)S(1)} %gather_fusion.13), channel_id=1, source_target_pairs={{1,0},{2,1},{3,2},{4,3},{5,4},{6,5},{7,6},{8,7},{9,8},{10,9},{11,1... | collective-permute-start | bytes 393224 | tf_op jit(solution)/shard_map/ppermute | solution.py:17
  451.7 43.6 %collective-permute-start.14 = (f32[128,256]{1,0:T(8,128)}, f32[128,256]{1,0:T(8,128)}, u32[]{:S(2)}, u32[]{:S(2)}) collective-permute-start(f32[128,256]{1,0:T(8,128)} %gather_fusion.14), channel_id=1, source_target_pairs={{0,1},{1,2},{2,3},{3,4},{4,5},{5,6},{6,7},{7,8},{8,9},{9,10},{10,1... | collective-permute-start | bytes 393224 | tf_op jit(solution)/shard_map/ppermute | solution.py:17
  455.8 41.6 %collective-permute-start.15 = (f32[128,256]{1,0:T(8,128)S(1)}, f32[128,256]{1,0:T(8,128)S(1)}, u32[]{:S(2)}, u32[]{:S(2)}) collective-permute-start(f32[128,256]{1,0:T(8,128)S(1)} %gather_fusion.15), channel_id=1, source_target_pairs={{1,0},{2,1},{3,2},{4,3},{5,4},{6,5},{7,6},{8,7},{9,8},{10,9},{11,1... | collective-permute-start | bytes 393224 | tf_op jit(solution)/shard_map/ppermute | solution.py:17
  499.1 2.6 copy-start.6
  509.8 74.4 %collective-permute-start.16 = (f32[128,256]{1,0:T(8,128)S(1)}, f32[128,256]{1,0:T(8,128)S(1)}, u32[]{:S(2)}, u32[]{:S(2)}) collective-permute-start(f32[128,256]{1,0:T(8,128)S(1)} %gather_fusion.16), channel_id=1, source_target_pairs={{0,1},{1,2},{2,3},{3,4},{4,5},{5,6},{6,7},{7,8},{8,9},{9,10},{10,1... | collective-permute-start | bytes 393224 | tf_op jit(solution)/shard_map/ppermute | solution.py:17
  514.5 71.4 %collective-permute-start.17 = (f32[128,256]{1,0:T(8,128)S(1)}, f32[128,256]{1,0:T(8,128)S(1)}, u32[]{:S(2)}, u32[]{:S(2)}) collective-permute-start(f32[128,256]{1,0:T(8,128)S(1)} %gather_fusion.17), channel_id=1, source_target_pairs={{1,0},{2,1},{3,2},{4,3},{5,4},{6,5},{7,6},{8,7},{9,8},{10,9},{11,1... | collective-permute-start | bytes 393224 | tf_op jit(solution)/shard_map/ppermute | solution.py:17
  587.6 32.8 %copy-start.2 = (f32[1024,256]{1,0:T(8,128)S(1)}, f32[1024,256]{1,0:T(8,128)}, u32[]{:S(2)}) copy-start(f32[1024,256]{1,0:T(8,128)} %copy-done.1) | copy-start | bytes 3145732
  587.6 32.8 %copy-start.5 = (f32[1024,256]{1,0:T(8,128)S(1)}, f32[1024,256]{1,0:T(8,128)}, u32[]{:S(2)}) copy-start(f32[1024,256]{1,0:T(8,128)} %copy-done.3) | copy-start | bytes 3145732
  (4 other events, 4.9 us)
